TPU v7x, 1024 devices: a whole 8x8x8 slice. The times are simulated.
1024 devices in a mesh: energy: 16 (over z, core), slab: 64 (over x, y).
Axes of the slice: x: 8, y: 8, z: 8, core: 2. Of those that a mesh axis runs over, the one named last changes fastest.
Arguments:
- green_less: bfloat16 [32, 64, 2, 256, 256], P('energy', 'slab'), may hold values from -6 to 6
- green_ret: bfloat16 [32, 64, 2, 256, 256], P('energy', 'slab'), may hold values from -0.375 to 0.375
- hamilton: bfloat16 [64, 256, 256], P('slab'), may hold values from -0.375 to 0.375
- coupling: bfloat16 [4, 256, 256], replicated, may hold values from -3 to 3
- occupation: float32 [4], replicated, may hold values from 0.2 to 2
- shifts: int32 [4], replicated, may hold values from 1 to 2, as said below
- interface: bfloat16 [2, 64, 64], replicated, may hold values from -0.75 to 0.75
Outputs:
- lesser_new: bfloat16 [32, 64, 2, 256, 256], P('energy', 'slab')
- chain: float32 [32, 64, 2, 64, 64], P('energy', 'slab')
Inputs may be any that keep to these rules, and one draw needn't show every extreme that they name: `shifts`: every mode's shift is a positive whole number of grid points, and some mode has shift 2.
All inputs are finite; a program needn't handle non-finite values.
Results may differ from a plain program's by a relative error of at most 0.0017.
The roundings to bfloat16 on the way count: a program that leaves them out, or rounds other values in their place, can miss the bound.
Values may be sent and summed in bfloat16 or wider, within the bound.
A program may use at most 32 MiB of HBM per device.

v0:
```python
import functools
import math

import jax
import jax.numpy as jnp
from jax import lax
from jax.experimental import pallas as pl
from jax.experimental.pallas import tpu as pltpu
from jax.sharding import PartitionSpec as P

NB = 64
MODES = 4
KSPAN = 2
ETA = 2.0
BF = jnp.bfloat16
F32 = jnp.float32
MESH = pl.DeviceIdType.MESH


def dot(a, b):
    return jnp.dot(a, b, preferred_element_type=F32)


def dot_t(a, b):
    return lax.dot_general(a, b, (((1,), (1,)), ((), ())), preferred_element_type=F32)


def halves(value):
    high = value.astype(BF)
    return high, (value - high.astype(F32)).astype(BF)


def lane_sign(rows):
    lane = lax.broadcasted_iota(jnp.int32, (rows, 2 * NB), 1)
    return jnp.where(lane < NB, -1.0, 1.0).astype(F32)


def times_i(value):
    return pltpu.roll(value, NB, 1) * lane_sign(value.shape[0])


def eye_pair():
    row = lax.broadcasted_iota(jnp.int32, (NB, 2 * NB), 0)
    lane = lax.broadcasted_iota(jnp.int32, (NB, 2 * NB), 1)
    return jnp.where(row == lane, 1.0, 0.0).astype(F32)


def cmul(a, b):
    full = jnp.concatenate([b, times_i(b)], 0)
    bh, bl = halves(full)
    ah, al = halves(a)
    left = jnp.concatenate([ah, al], 1)
    both = jnp.concatenate([bh, bl], 1)
    right = jnp.concatenate([both, both], 0)
    out = dot(left, right)
    return out[:, : 2 * NB] + out[:, 2 * NB :]


def kernel(
    ng, nx, ny, orb,
    less, ret, ham, coup, occ, shf, face,
    lesser, chain,
    grn, rv, hv, cv, coef, sig, half, new, brow, tcol, facev, pre, outv,
    local_sem, halo_s, halo_r, y_s, y_r, x_s, x_r,
):
    g = lax.axis_index("energy")
    s = lax.axis_index("slab")
    x = lax.div(s, ny)
    y = lax.rem(s, ny)
    slab_y = lambda d: x * ny + lax.rem(y + d + ny, ny)
    slab_x = lambda d: lax.rem(x + d + nx, nx) * ny + y

    own_copy = pltpu.make_async_copy(less.at[:, 0], grn.at[1], local_sem.at[0])
    cv_copy = pltpu.make_async_copy(coup, cv, local_sem.at[1])
    hv_copy = pltpu.make_async_copy(ham.at[0], hv, local_sem.at[2])
    rv_copy = pltpu.make_async_copy(ret.at[:, 0], rv, local_sem.at[3])
    for c in (own_copy, cv_copy, hv_copy, rv_copy):
        c.start()

    barrier = pltpu.get_barrier_semaphore()
    peers = [
        (lax.rem(g + 1, ng), s),
        (lax.rem(g + ng - 1, ng), s),
        (g, slab_y(1)),
        (g, slab_y(-1)),
        (g, slab_x(1)),
        (g, slab_x(-1)),
    ]
    for peer in peers:
        pl.semaphore_signal(barrier, inc=1, device_id=peer, device_id_type=MESH)
    pl.semaphore_wait(barrier, len(peers))

    regions = [
        (pl.ds(0, NB), pl.ds(0, orb)),
        (pl.ds(NB, orb - NB), pl.ds(0, 2 * NB)),
        (pl.ds(NB, orb - NB), pl.ds(2 * NB, orb - 2 * NB)),
    ]

    def halo(side, part):
        rows, cols = regions[part]
        to = lax.rem(g + 1, ng) if side == 0 else lax.rem(g + ng - 1, ng)
        return pltpu.make_async_remote_copy(
            src_ref=less.at[:, 0, :, rows, cols],
            dst_ref=grn.at[0 if side == 0 else 2, :, :, rows, cols],
            send_sem=halo_s.at[side, part],
            recv_sem=halo_r.at[side, part],
            device_id=(to, s),
            device_id_type=MESH,
        )

    for part in range(3):
        @pl.when(g < ng - 1)
        def _():
            halo(0, part).start()

        @pl.when(g > 0)
        def _():
            halo(1, part).start()

    @pl.when(g == 0)
    def _():
        grn[0] = jnp.zeros(grn.shape[1:], BF)

    @pl.when(g == ng - 1)
    def _():
        grn[2] = jnp.zeros(grn.shape[1:], BF)

    cv_copy.wait()
    up_w, low_w = [], []
    for m in range(MODES):
        n = occ[m]
        two = (shf[m] - 1).astype(F32)
        one = 1.0 - two
        up_w.append(((n + 1.0) * one, (n + 1.0) * two))
        low_w.append((n * one, n * two))

    def coef_rows(i, _):
        rows = pl.ds(pl.multiple_of(i * 16, 16), 16)
        planes = [cv[m, rows, :].astype(F32) for m in range(MODES)]
        for k in range(2):
            coef[k, rows, :] = sum(planes[m] * up_w[m][k] for m in range(MODES))
            coef[2 + k, rows, :] = sum(planes[m] * low_w[m][k] for m in range(MODES))
        return 0

    lax.fori_loop(0, orb // 16, coef_rows, 0)

    face_row = jnp.concatenate([face[0].astype(F32), face[1].astype(F32)], 1)
    facev[...] = jnp.concatenate([face_row, times_i(face_row)], 0).astype(BF)

    hv_copy.wait()
    row_i = lax.broadcasted_iota(jnp.int32, (orb, orb), 0)
    col_i = lax.broadcasted_iota(jnp.int32, (orb, orb), 1)
    diag_h = jnp.sum(jnp.where(row_i == col_i, hv[...].astype(F32), 0.0), axis=0, keepdims=True)
    inner = lax.broadcasted_iota(jnp.int32, (1, orb), 1) >= NB
    inverse = []
    for e in range(2):
        energy = -3.0 + 6.0 * ((2 * g + e).astype(F32) + 0.5) * (1.0 / (2 * ng))
        offset = energy - diag_h
        denom = offset * offset + ETA * ETA
        inverse.append((jnp.where(inner, offset / denom, 0.0), jnp.where(inner, -ETA / denom, 0.0)))

    own_copy.wait()

    def halo_wait(part):
        @pl.when(g > 0)
        def _():
            halo(0, part).wait_recv()

        @pl.when(g < ng - 1)
        def _():
            halo(1, part).wait_recv()

    def sigma_region(first, count, cols):
        def body(i, _):
            rows = pl.ds(pl.multiple_of(first + i * 16, 16), 16)
            a1, a2, b1, b2 = [coef[k, rows, cols] for k in range(4)]
            for c in range(2):
                field = [grn[f // 2, f % 2, c, rows, cols].astype(F32) for f in range(6)]
                for e in range(2):
                    total = a1 * field[e + 3] + a2 * field[e + 4] + b1 * field[e + 1] + b2 * field[e]
                    sig[e, c, rows, cols] = total.astype(BF)
            return 0

        lax.fori_loop(0, count // 16, body, 0)

    halo_wait(0)
    sigma_region(0, NB, pl.ds(0, orb))
    halo_wait(1)
    sigma_region(NB, orb - NB, pl.ds(0, 2 * NB))

    lane256 = lax.broadcasted_iota(jnp.int32, (orb, 2 * NB), 1)
    for e in range(2):
        top_r = hv[0:NB, :].astype(F32) + sig[e, 0, 0:NB, :].astype(F32)
        top_i = sig[e, 1, 0:NB, :].astype(F32)
        inv_r, inv_i = inverse[e]
        q_r = (top_r * inv_r - top_i * inv_i).astype(BF)
        q_i = (top_r * inv_i + top_i * inv_r).astype(BF)
        left_r = hv[:, 0 : 2 * NB].astype(F32) + sig[e, 0, :, 0 : 2 * NB].astype(F32)
        left_i = pltpu.roll(sig[e, 1, :, 0 : 2 * NB].astype(F32), NB, 1)
        pair = jnp.where(lane256 < NB, left_r, left_i)
        prod = dot(jnp.concatenate([q_r, q_i], 0), pair.astype(BF))
        bound = pair[0:NB] - (prod[0:NB] + times_i(prod[NB:]))
        brow[y, e] = bound.astype(BF)

    def hop(buf, sems, recvs, e, way, step, n, pos, to):
        idx = lax.rem(pos - (step - 1) + n, n) if way == 0 else lax.rem(pos + (step - 1), n)
        return pltpu.make_async_remote_copy(
            src_ref=buf.at[idx, e],
            dst_ref=buf.at[idx, e],
            send_sem=sems.at[way, step - 1, e],
            recv_sem=recvs.at[way, step - 1, e],
            device_id=(g, to),
            device_id_type=MESH,
        )

    def hop_y(e, way, step):
        return hop(brow, y_s, y_r, e, way, step, ny, y, slab_y(1 if way == 0 else -1))

    def hop_x(e, way, step):
        return hop(tcol, x_s, x_r, e, way, step, nx, x, slab_x(1 if way == 0 else -1))

    def reach(n):
        return n // 2, n // 2 - 1

    def ring(hopper, n, on_arrival, fill):
        ways = reach(n)
        for step in range(1, ways[0] + 1):
            for e in range(2):
                for way in range(2):
                    if step <= ways[way]:
                        hopper(e, way, step).wait_recv()
                        if step < ways[way]:
                            hopper(e, way, step + 1).start()
            for e in range(2):
                for way in range(2):
                    if step <= ways[way]:
                        on_arrival(e, way, step)
            if step < ways[0]:
                fill(step)

    def start_ring(hopper, n, e):
        for way in range(2):
            if reach(n)[way] > 0:
                hopper(e, way, 1).start()

    scale = 1.0 / (8.0 * math.sqrt(NB * nx * ny))

    def factor(idx, e):
        return eye_pair() + scale * dot(brow[idx, e], facev[...])

    for e in range(2):
        start_ring(hop_y, ny, e)

    def rest_of_sigma():
        halo_wait(2)
        sigma_region(NB, orb - NB, pl.ds(2 * NB, orb - 2 * NB))

    def half_block(e):
        rr, ri = rv[e, 0], rv[e, 1]
        sr, si = sig[e, 0], sig[e, 1]
        half[e, 0] = (dot(rr, sr) - dot(ri, si)).astype(BF)
        half[e, 1] = (dot(rr, si) + dot(ri, sr)).astype(BF)

    def new_block(e):
        rr, ri = rv[e, 0], rv[e, 1]
        hr, hi = half[e, 0], half[e, 1]
        new[e, 0] = (dot_t(hr, rr) + dot_t(hi, ri)).astype(BF)
        new[e, 1] = (dot_t(hi, rr) - dot_t(hr, ri)).astype(BF)
        out_copy(e).start()

    def out_copy(e):
        return pltpu.make_async_copy(new.at[e], lesser.at[e, 0], local_sem.at[4 + e])

    rest_of_sigma()
    rv_copy.wait()

    eye = eye_pair()
    prefix = [factor(y, e) for e in range(2)]
    wrapped = [eye, eye]
    suffix_a = [eye, eye]
    suffix_b = [eye, eye]

    def arrive_y(e, way, step):
        if way == 0:
            idx = lax.rem(y - step + ny, ny)
            mine = y - step >= 0
            product = cmul(factor(idx, e), jnp.where(mine, prefix[e], suffix_b[e]))
            prefix[e] = jnp.where(mine, product, prefix[e])
            suffix_b[e] = jnp.where(mine, suffix_b[e], product)
        else:
            idx = lax.rem(y + step, ny)
            after = y + step < ny
            product = cmul(jnp.where(after, suffix_a[e], wrapped[e]), factor(idx, e))
            suffix_a[e] = jnp.where(after, product, suffix_a[e])
            wrapped[e] = jnp.where(after, wrapped[e], product)

    def fill_y(step):
        if step == 1:
            half_block(0)
        elif step == 2:
            half_block(1)

    ring(hop_y, ny, arrive_y, fill_y)
    for e in range(2):
        before = cmul(wrapped[e], prefix[e])
        tcol[x, e] = cmul(before, cmul(suffix_a[e], suffix_b[e]))
        pre[e] = before
        start_ring(hop_x, nx, e)

    if reach(ny)[0] < 3:
        half_block(1)
    if reach(ny)[0] < 2:
        half_block(0)

    total = [pre[0], pre[1]]
    outer = [eye, eye]

    def arrive_x(e, way, step):
        if way == 0:
            idx = lax.rem(x - step + nx, nx)
            block = jnp.where(x - step >= 0, tcol[idx, e], eye)
            total[e] = cmul(block, total[e])
        else:
            idx = lax.rem(x + step, nx)
            block = jnp.where(x + step >= nx, tcol[idx, e], eye)
            outer[e] = cmul(outer[e], block)

    def fill_x(step):
        if step == 1:
            new_block(0)
        elif step == 2:
            new_block(1)

    ring(hop_x, nx, arrive_x, fill_x)
    if reach(nx)[0] < 3:
        new_block(1)
    if reach(nx)[0] < 2:
        new_block(0)

    chain_copies = []
    for e in range(2):
        whole = cmul(outer[e], total[e])
        outv[e, 0] = whole[:, 0:NB]
        outv[e, 1] = pltpu.roll(whole, NB, 1)[:, 0:NB]
        copy = pltpu.make_async_copy(outv.at[e], chain.at[e, 0], local_sem.at[6 + e])
        copy.start()
        chain_copies.append(copy)

    for part in range(3):
        @pl.when(g < ng - 1)
        def _():
            halo(0, part).wait_send()

        @pl.when(g > 0)
        def _():
            halo(1, part).wait_send()

    for hopper, n in ((hop_y, ny), (hop_x, nx)):
        for way in range(2):
            for step in range(1, reach(n)[way] + 1):
                for e in range(2):
                    hopper(e, way, step).wait_send()
    for e in range(2):
        out_copy(e).wait()
        chain_copies[e].wait()


def solution(mesh, grid=None):
    ng, ns = mesh.shape["energy"], mesh.shape["slab"]
    nx, ny = grid or (math.isqrt(ns), ns // math.isqrt(ns))

    def on_device(less, ret, ham, coup, occ, shf, face):
        e_count, orb = less.shape[0], less.shape[3]
        any_space = pl.BlockSpec(memory_space=pl.ANY)
        smem = pl.BlockSpec(memory_space=pltpu.SMEM)
        vmem = pl.BlockSpec(memory_space=pltpu.VMEM)
        reach_y, reach_x = max(ny // 2, 1), max(nx // 2, 1)
        dma = pltpu.SemaphoreType.DMA
        return pl.pallas_call(
            functools.partial(kernel, ng, nx, ny, orb),
            out_shape=(
                jax.ShapeDtypeStruct((e_count, 1, 2, orb, orb), BF),
                jax.ShapeDtypeStruct((e_count, 1, 2, NB, NB), F32),
            ),
            in_specs=[any_space, any_space, any_space, any_space, smem, smem, vmem],
            out_specs=(any_space, any_space),
            scratch_shapes=[
                pltpu.VMEM((3, 2, 2, orb, orb), BF),
                pltpu.VMEM((2, 2, orb, orb), BF),
                pltpu.VMEM((orb, orb), BF),
                pltpu.VMEM((MODES, orb, orb), BF),
                pltpu.VMEM((4, orb, orb), F32),
                pltpu.VMEM((2, 2, orb, orb), BF),
                pltpu.VMEM((2, 2, orb, orb), BF),
                pltpu.VMEM((2, 2, orb, orb), BF),
                pltpu.VMEM((ny, 2, NB, 2 * NB), BF),
                pltpu.VMEM((nx, 2, NB, 2 * NB), F32),
                pltpu.VMEM((2 * NB, 2 * NB), BF),
                pltpu.VMEM((2, NB, 2 * NB), F32),
                pltpu.VMEM((2, 2, NB, NB), F32),
                dma((8,)),
                dma((2, 3)),
                dma((2, 3)),
                dma((2, reach_y, 2)),
                dma((2, reach_y, 2)),
                dma((2, reach_x, 2)),
                dma((2, reach_x, 2)),
            ],
            compiler_params=pltpu.CompilerParams(collective_id=0, has_side_effects=True),
        )(less, ret, ham, coup, occ, shf, face)

    in_specs = (
        P("energy", "slab", None, None, None),
        P("energy", "slab", None, None, None),
        P("slab", None, None),
        P(),
        P(),
        P(),
        P(),
    )
    out_specs = (P("energy", "slab", None, None, None), P("energy", "slab", None, None, None))
    return jax.shard_map(on_device, mesh=mesh, in_specs=in_specs, out_specs=out_specs, check_vma=False)
```

profile of v0, /device:TPU:2, one launch (start us, length us, event | category | flops | bytes accessed | tf_op | source)
XLA Modules:
  0.0 54.1 jit_solution(12279773961796260342)
XLA Ops:
  0.6 50.9 %shard_map.86 = (bf16[2,1,2,256,256]{4,3,2,1,0:T(8,128)(2,1)}, f32[2,1,2,64,64]{4,3,2,1,0:T(8,128)}) custom-call(bf16[2,1,2,256,256]{4,3,2,1,0:T(8,128)(2,1)} %less.1, bf16[2,1,2,256,256]{4,3,2,1,0:T(8,128)(2,1)} %ret.1, bf16[1,256,256]{2,1,0:T(8,128)(2,1)} %ham.1, bf16[4,256,256]{2,1,0:T(8,128)(2,1)} %coup.1, f32[4]{0:T(128)} %occ.1, s32[4]{0:T(128)} %shf.1, ...), custom_call_target="tpu_custom_call" | custom-call | tf_op jit(solution)/shard_map/pallas_call | solution.py:379
  51.5 0.0 copy-start
  51.5 1.9 %copy.11 = bf16[2,1,2,256,256]{4,3,2,1,0:T(8,128)(2,1)} copy(bf16[2,1,2,256,256]{4,3,2,1,0:T(8,128)(2,1)} %get-tuple-element.4) | data formatting | bytes 1048576
  53.4 0.0 copy-done
  53.4 0.7 %copy.12 = f32[2,1,2,64,64]{4,3,2,1,0:T(8,128)} copy(f32[2,1,2,64,64]{4,3,2,1,0:T(8,128)S(1)} %copy-done) | data formatting | bytes 131072
Async XLA Ops:
  51.5 1.9 %copy-start = (f32[2,1,2,64,64]{4,3,2,1,0:T(8,128)S(1)}, f32[2,1,2,64,64]{4,3,2,1,0:T(8,128)}, u32[]{:S(2)}) copy-start(f32[2,1,2,64,64]{4,3,2,1,0:T(8,128)} %get-tuple-element.5) | copy-start | bytes 196612
where the time goes:
time: 54.3 us; the launch traced here: 54.1 us
  Pallas kernels  50.9 us (94%)
  local copies, waits for them, and re-layouts  2.56 us (5%)
  between operations  0.65 us (1%)
    pallas_call x1, Pallas kernels, on_device(): pl.pallas_call(functools.partial(kernel, ng, nx, ny, orb), out_shape=(jax...  50.9 us
    unnamed x4, local copies, waits for them, and re-layouts  2.56 us

commit v1 on v0

v1 whole, which is shorter than its diff:
```python
import functools
import math

import jax
import jax.numpy as jnp
from jax import lax
from jax.experimental import pallas as pl
from jax.experimental.pallas import tpu as pltpu
from jax.sharding import PartitionSpec as P

NB = 64
MODES = 4
KSPAN = 2
ETA = 2.0
BF = jnp.bfloat16
F32 = jnp.float32
MESH = pl.DeviceIdType.MESH


def dot(a, b):
    return jnp.dot(a, b, preferred_element_type=F32)


def dot_t(a, b):
    return lax.dot_general(a, b, (((1,), (1,)), ((), ())), preferred_element_type=F32)


def halves(value):
    high = value.astype(BF)
    return high, (value - high.astype(F32)).astype(BF)


def lane_sign(rows):
    lane = lax.broadcasted_iota(jnp.int32, (rows, 2 * NB), 1)
    return jnp.where(lane < NB, -1.0, 1.0).astype(F32)


def times_i(value):
    return pltpu.roll(value, NB, 1) * lane_sign(value.shape[0])


def eye_pair():
    row = lax.broadcasted_iota(jnp.int32, (NB, 2 * NB), 0)
    lane = lax.broadcasted_iota(jnp.int32, (NB, 2 * NB), 1)
    return jnp.where(row == lane, 1.0, 0.0).astype(F32)


def cmul(a, b):
    full = jnp.concatenate([b, times_i(b)], 0)
    bh, bl = halves(full)
    ah, al = halves(a)
    left = jnp.concatenate([ah, al], 1)
    both = jnp.concatenate([bh, bl], 1)
    right = jnp.concatenate([both, both], 0)
    out = dot(left, right)
    return out[:, : 2 * NB] + out[:, 2 * NB :]


def kernel(
    ng, nx, ny, orb,
    less, ret, ham, coup, occ, shf, face,
    lesser, chain,
    grn, rv, hv, cv, coef, sig, half, brow, tcol, facev, pre, swap,
    local_sem, ready, halo_s, halo_r, y_s, y_r, x_s, x_r, swap_s, swap_r,
):
    g = lax.axis_index("energy")
    s = lax.axis_index("slab")
    x = lax.div(s, ny)
    y = lax.rem(s, ny)
    slab_y = lambda d: x * ny + lax.rem(y + d + ny, ny)
    slab_x = lambda d: lax.rem(x + d + nx, nx) * ny + y
    mine = lax.rem(y, 2)
    other = 1 - mine

    own_copy = pltpu.make_async_copy(less.at[:, 0], grn.at[1], local_sem.at[0])
    cv_copy = pltpu.make_async_copy(coup, cv, local_sem.at[1])
    hv_copy = pltpu.make_async_copy(ham.at[0], hv, local_sem.at[2])
    rv_copy = pltpu.make_async_copy(ret.at[:, 0], rv, local_sem.at[3])
    for c in (cv_copy, own_copy, hv_copy, rv_copy):
        c.start()

    barrier = pltpu.get_barrier_semaphore()
    around = [slab_y(1), slab_y(-1), slab_x(1), slab_x(-1)]
    peers = [(lax.rem(g + 1, ng), s), (lax.rem(g + ng - 1, ng), s)] + [(g, p) for p in around]
    for peer in peers:
        pl.semaphore_signal(barrier, inc=1, device_id=peer, device_id_type=MESH)
    pl.semaphore_wait(barrier, len(peers))

    last_round = max(nx, ny) // 2

    def tell(r):
        if 2 <= r <= last_round:
            for way, p in enumerate(around):
                pl.semaphore_signal(ready.at[way, r - 2], inc=1, device_id=(g, p), device_id_type=MESH)

    def hear(r):
        if 2 <= r <= last_round:
            for way in range(4):
                pl.semaphore_wait(ready.at[way, r - 2], 1)

    regions = [
        (pl.ds(0, NB), pl.ds(0, orb)),
        (pl.ds(NB, orb - NB), pl.ds(0, 2 * NB)),
        (pl.ds(NB, orb - NB), pl.ds(2 * NB, orb - 2 * NB)),
    ]

    def halo(side, part):
        rows, cols = regions[part]
        to = lax.rem(g + 1, ng) if side == 0 else lax.rem(g + ng - 1, ng)
        return pltpu.make_async_remote_copy(
            src_ref=less.at[:, 0, :, rows, cols],
            dst_ref=grn.at[0 if side == 0 else 2, :, :, rows, cols],
            send_sem=halo_s.at[side, part],
            recv_sem=halo_r.at[side, part],
            device_id=(to, s),
            device_id_type=MESH,
        )

    for part in range(3):
        @pl.when(g < ng - 1)
        def _():
            halo(0, part).start()

        @pl.when(g > 0)
        def _():
            halo(1, part).start()

    tell(2)

    @pl.when(g == 0)
    def _():
        grn[0] = jnp.zeros(grn.shape[1:], BF)

    @pl.when(g == ng - 1)
    def _():
        grn[2] = jnp.zeros(grn.shape[1:], BF)

    cv_copy.wait()
    up_w, low_w = [], []
    for m in range(MODES):
        n = occ[m]
        two = (shf[m] - 1).astype(F32)
        one = 1.0 - two
        up_w.append(((n + 1.0) * one, (n + 1.0) * two))
        low_w.append((n * one, n * two))

    def coef_rows(i, _):
        rows = pl.ds(pl.multiple_of(i * 16, 16), 16)
        planes = [cv[m, rows, :].astype(F32) for m in range(MODES)]
        for k in range(2):
            coef[k, rows, :] = sum(planes[m] * up_w[m][k] for m in range(MODES))
            coef[2 + k, rows, :] = sum(planes[m] * low_w[m][k] for m in range(MODES))
        return 0

    lax.fori_loop(0, orb // 16, coef_rows, 0)
    hear(2)
    tell(3)

    face_row = jnp.concatenate([face[0].astype(F32), face[1].astype(F32)], 1)
    facev[...] = jnp.concatenate([face_row, times_i(face_row)], 0).astype(BF)

    hv_copy.wait()
    row_i = lax.broadcasted_iota(jnp.int32, (orb, orb), 0)
    col_i = lax.broadcasted_iota(jnp.int32, (orb, orb), 1)
    diag_h = jnp.sum(jnp.where(row_i == col_i, hv[...].astype(F32), 0.0), axis=0, keepdims=True)
    inner = lax.broadcasted_iota(jnp.int32, (1, orb), 1) >= NB
    inverse = []
    for e in range(2):
        energy = -3.0 + 6.0 * ((2 * g + e).astype(F32) + 0.5) * (1.0 / (2 * ng))
        offset = energy - diag_h
        denom = offset * offset + ETA * ETA
        inverse.append((jnp.where(inner, offset / denom, 0.0), jnp.where(inner, -ETA / denom, 0.0)))

    own_copy.wait()
    hear(3)
    tell(4)

    def halo_wait(part):
        @pl.when(g > 0)
        def _():
            halo(0, part).wait_recv()

        @pl.when(g < ng - 1)
        def _():
            halo(1, part).wait_recv()

    def sigma_region(first, count, cols):
        def body(i, _):
            rows = pl.ds(pl.multiple_of(first + i * 16, 16), 16)
            a1, a2, b1, b2 = [coef[k, rows, cols] for k in range(4)]
            for c in range(2):
                field = [grn[f // 2, f % 2, c, rows, cols].astype(F32) for f in range(6)]
                for e in range(2):
                    total = a1 * field[e + 3] + a2 * field[e + 4] + b1 * field[e + 1] + b2 * field[e]
                    sig[e, c, rows, cols] = total.astype(BF)
            return 0

        lax.fori_loop(0, count // 16, body, 0)

    halo_wait(0)
    sigma_region(0, NB, pl.ds(0, orb))
    halo_wait(1)
    sigma_region(NB, orb - NB, pl.ds(0, 2 * NB))

    lane256 = lax.broadcasted_iota(jnp.int32, (orb, 2 * NB), 1)
    for e in range(2):
        top_r = hv[0:NB, :].astype(F32) + sig[e, 0, 0:NB, :].astype(F32)
        top_i = sig[e, 1, 0:NB, :].astype(F32)
        inv_r, inv_i = inverse[e]
        q_r = (top_r * inv_r - top_i * inv_i).astype(BF)
        q_i = (top_r * inv_i + top_i * inv_r).astype(BF)
        left_r = hv[:, 0 : 2 * NB].astype(F32) + sig[e, 0, :, 0 : 2 * NB].astype(F32)
        left_i = pltpu.roll(sig[e, 1, :, 0 : 2 * NB].astype(F32), NB, 1)
        pair = jnp.where(lane256 < NB, left_r, left_i)
        prod = dot(jnp.concatenate([q_r, q_i], 0), pair.astype(BF))
        bound = pair[0:NB] - (prod[0:NB] + times_i(prod[NB:]))
        brow[e, y] = bound.astype(BF)

    for r in range(4, last_round + 1):
        hear(r)
        tell(r + 1)

    far_first = lambda n: sorted(range(1, n), key=lambda d: -min(d, n - d))

    def row_send(d, first):
        to = lax.rem(y + d, ny)
        e = lax.rem(to, 2) if first else 1 - lax.rem(to, 2)
        return pltpu.make_async_remote_copy(
            src_ref=brow.at[e, y],
            dst_ref=brow.at[e, y],
            send_sem=y_s.at[0 if first else 1, d - 1],
            recv_sem=y_r.at[0 if first else 1, y],
            device_id=(g, slab_y(d)),
            device_id_type=MESH,
        )

    def row_wait(source, first):
        e = mine if first else other
        pltpu.make_async_remote_copy(
            src_ref=brow.at[e, source],
            dst_ref=brow.at[e, source],
            send_sem=y_s.at[0 if first else 1, 0],
            recv_sem=y_r.at[0 if first else 1, source],
            device_id=(g, slab_y(1)),
            device_id_type=MESH,
        ).wait_recv()

    for d in far_first(ny):
        row_send(d, True).start()
    for d in far_first(ny):
        @pl.when(y + d < ny)
        def _():
            row_send(d, False).start()

    halo_wait(2)
    sigma_region(NB, orb - NB, pl.ds(2 * NB, orb - 2 * NB))
    rv_copy.wait()
    for e in range(2):
        rr, ri = rv[e, 0], rv[e, 1]
        sr, si = sig[e, 0], sig[e, 1]
        half[e, 0] = (dot(rr, sr) - dot(ri, si)).astype(BF)
        half[e, 1] = (dot(rr, si) + dot(ri, sr)).astype(BF)
    for e in range(2):
        rr, ri = rv[e, 0], rv[e, 1]
        hr, hi = half[e, 0], half[e, 1]
        lesser[e, 0, 0] = (dot_t(hr, rr) + dot_t(hi, ri)).astype(BF)
        lesser[e, 0, 1] = (dot_t(hi, rr) - dot_t(hr, ri)).astype(BF)

    scale = 1.0 / (8.0 * math.sqrt(NB * nx * ny))
    eye = eye_pair()

    def factors(e):
        rows = dot(brow[e].reshape(ny * NB, 2 * NB), facev[...])
        return [eye + scale * rows[i * NB : (i + 1) * NB] for i in range(ny)]

    def ordered_product(blocks):
        while len(blocks) > 1:
            pairs = [cmul(blocks[i], blocks[i + 1]) for i in range(0, len(blocks) - 1, 2)]
            blocks = pairs + blocks[len(blocks) - len(blocks) % 2 :]
        return blocks[0]

    for d in range(1, ny):
        row_wait(lax.rem(y + d, ny), True)
    tcol[x] = ordered_product(factors(mine))

    def total_send(d):
        return pltpu.make_async_remote_copy(
            src_ref=tcol.at[x],
            dst_ref=tcol.at[x],
            send_sem=x_s.at[d - 1],
            recv_sem=x_r.at[x],
            device_id=(g, slab_x(d)),
            device_id_type=MESH,
        )

    for d in far_first(nx):
        @pl.when(x + d < nx)
        def _():
            total_send(d).start()

    for d in range(1, ny):
        @pl.when(y - d >= 0)
        def _():
            row_wait(lax.rem(y - d + ny, ny), False)
    for e in range(2):
        pre[e] = ordered_product([jnp.where(i <= y, f, eye) for i, f in enumerate(factors(e))])

    for d in range(1, nx):
        @pl.when(x - d >= 0)
        def _():
            source = lax.rem(x - d + nx, nx)
            pltpu.make_async_remote_copy(
                src_ref=tcol.at[source],
                dst_ref=tcol.at[source],
                send_sem=x_s.at[0],
                recv_sem=x_r.at[source],
                device_id=(g, slab_x(1)),
                device_id_type=MESH,
            ).wait_recv()
    swap[0] = ordered_product([jnp.where(i < x, tcol[i], eye) for i in range(nx - 1)])
    swap_copy = pltpu.make_async_remote_copy(
        src_ref=swap.at[0],
        dst_ref=swap.at[1],
        send_sem=swap_s.at[0],
        recv_sem=swap_r.at[0],
        device_id=(g, slab_y(1 - 2 * mine)),
        device_id_type=MESH,
    )
    swap_copy.start()

    def finish(e, rows_before):
        whole = cmul(rows_before, pre[e])
        chain[e, 0, 0] = whole[:, 0:NB]
        chain[e, 0, 1] = pltpu.roll(whole, NB, 1)[:, 0:NB]

    finish(mine, swap[0])

    for part in range(3):
        @pl.when(g < ng - 1)
        def _():
            halo(0, part).wait_send()

        @pl.when(g > 0)
        def _():
            halo(1, part).wait_send()

    for d in range(1, ny):
        row_send(d, True).wait_send()

        @pl.when(y + d < ny)
        def _():
            row_send(d, False).wait_send()

    for d in range(1, nx):
        @pl.when(x + d < nx)
        def _():
            total_send(d).wait_send()

    swap_copy.wait()
    finish(other, swap[1])


def solution(mesh, grid=None):
    ng, ns = mesh.shape["energy"], mesh.shape["slab"]
    nx, ny = grid or (math.isqrt(ns), ns // math.isqrt(ns))

    def on_device(less, ret, ham, coup, occ, shf, face):
        e_count, orb = less.shape[0], less.shape[3]
        any_space = pl.BlockSpec(memory_space=pl.ANY)
        smem = pl.BlockSpec(memory_space=pltpu.SMEM)
        vmem = pl.BlockSpec(memory_space=pltpu.VMEM)
        dma = pltpu.SemaphoreType.DMA
        rounds = max(max(nx, ny) // 2 - 1, 1)
        return pl.pallas_call(
            functools.partial(kernel, ng, nx, ny, orb),
            out_shape=(
                pltpu.VMEM((e_count, 1, 2, orb, orb), BF),
                pltpu.VMEM((e_count, 1, 2, NB, NB), F32),
            ),
            in_specs=[any_space, any_space, any_space, any_space, smem, smem, vmem],
            out_specs=(vmem, vmem),
            scratch_shapes=[
                pltpu.VMEM((3, 2, 2, orb, orb), BF),
                pltpu.VMEM((2, 2, orb, orb), BF),
                pltpu.VMEM((orb, orb), BF),
                pltpu.VMEM((MODES, orb, orb), BF),
                pltpu.VMEM((4, orb, orb), F32),
                pltpu.VMEM((2, 2, orb, orb), BF),
                pltpu.VMEM((2, 2, orb, orb), BF),
                pltpu.VMEM((2, ny, NB, 2 * NB), BF),
                pltpu.VMEM((nx, NB, 2 * NB), F32),
                pltpu.VMEM((2 * NB, 2 * NB), BF),
                pltpu.VMEM((2, NB, 2 * NB), F32),
                pltpu.VMEM((2, NB, 2 * NB), F32),
                dma((4,)),
                pltpu.SemaphoreType.REGULAR((4, rounds)),
                dma((2, 3)),
                dma((2, 3)),
                dma((2, ny - 1)),
                dma((2, ny)),
                dma((nx - 1,)),
                dma((nx,)),
                dma((1,)),
                dma((1,)),
            ],
            compiler_params=pltpu.CompilerParams(collective_id=0, has_side_effects=True),
        )(less, ret, ham, coup, occ, shf, face)

    in_specs = (
        P("energy", "slab", None, None, None),
        P("energy", "slab", None, None, None),
        P("slab", None, None),
        P(),
        P(),
        P(),
        P(),
    )
    out_specs = (P("energy", "slab", None, None, None), P("energy", "slab", None, None, None))
    return jax.shard_map(on_device, mesh=mesh, in_specs=in_specs, out_specs=out_specs, check_vma=False)
```

time: 54.3 us -> 42.9 us (0.79)
  the two profiles are of different devices: /device:TPU:2 before, /device:TPU:14 now
where the time goes in v1:
time: 42.9 us; the launch traced here: 42.7 us
  Pallas kernels  40.6 us (95%)
  local copies, waits for them, and re-layouts  1.45 us (3%)
  between operations  0.64 us (1%)
    pallas_call x1, Pallas kernels, on_device(): pl.pallas_call(functools.partial(kernel, ng, nx, ny, orb), out_shape=(plt...  40.6 us
    unnamed x2, local copies, waits for them, and re-layouts  1.45 us

profile of v1, /device:TPU:14, one launch (start us, length us, event | category | flops | bytes accessed | tf_op | source)
XLA Modules:
  0.0 42.7 jit_solution(13893946079469225915)
XLA Ops:
  0.6 40.6 %shard_map.86 = (bf16[2,1,2,256,256]{4,3,2,1,0:T(8,128)(2,1)S(1)}, f32[2,1,2,64,64]{4,3,2,1,0:T(8,128)S(1)}) custom-call(bf16[2,1,2,256,256]{4,3,2,1,0:T(8,128)(2,1)} %less.1, bf16[2,1,2,256,256]{4,3,2,1,0:T(8,128)(2,1)} %ret.1, bf16[1,256,256]{2,1,0:T(8,128)(2,1)} %ham.1, bf16[4,256,256]{2,1,0:T(8,128)(2,1)} %coup.1, f32[4]{0:T(128)} %occ.1, s32[4]{0:T(128)} %shf.1, ...), custom_call_target="tpu_custom_call" | custom-call | tf_op jit(solution)/shard_map/pallas_call | solution.py:374
  41.2 0.8 %copy.11 = bf16[2,1,2,256,256]{4,3,2,1,0:T(8,128)(2,1)} copy(bf16[2,1,2,256,256]{4,3,2,1,0:T(8,128)(2,1)S(1)} %get-tuple-element.2) | data formatting | bytes 1048576
  42.0 0.7 %copy.12 = f32[2,1,2,64,64]{4,3,2,1,0:T(8,128)} copy(f32[2,1,2,64,64]{4,3,2,1,0:T(8,128)S(1)} %get-tuple-element.3) | data formatting | bytes 131072

commit v2 on v1

--- a/solution.py
+++ b/solution.py
@@ -12,6 +12,7 @@
 MODES = 4
 KSPAN = 2
 ETA = 2.0
+LATE = 2
 BF = jnp.bfloat16
 F32 = jnp.float32
 MESH = pl.DeviceIdType.MESH
@@ -60,8 +61,8 @@
     ng, nx, ny, orb,
     less, ret, ham, coup, occ, shf, face,
     lesser, chain,
-    grn, rv, hv, cv, coef, sig, half, brow, tcol, facev, pre, swap,
-    local_sem, ready, halo_s, halo_r, y_s, y_r, x_s, x_r, swap_s, swap_r,
+    grn, rv, hv, cv, coef, sig, half, brow, tcol, facev, pre, before, first_b,
+    local_sem, ready, hello, halo_s, halo_r, y_s, y_r, x_s, x_r, swap_s, swap_r, first_s, first_r,
 ):
     g = lax.axis_index("energy")
     s = lax.axis_index("slab")
@@ -79,24 +80,66 @@
     for c in (cv_copy, own_copy, hv_copy, rv_copy):
         c.start()
 
+    late = g < LATE
+    slab0 = s == 0
+    late0 = late & slab0
+    device0 = (g == 0) & slab0
+    line_y = late & (x == 0)
+    line_x = late & (y == 0)
+
     barrier = pltpu.get_barrier_semaphore()
+
+    def greet(to, cond):
+        @pl.when(cond)
+        def _():
+            pl.semaphore_signal(barrier, inc=1, device_id=to, device_id_type=MESH)
+
     around = [slab_y(1), slab_y(-1), slab_x(1), slab_x(-1)]
-    peers = [(lax.rem(g + 1, ng), s), (lax.rem(g + ng - 1, ng), s)] + [(g, p) for p in around]
-    for peer in peers:
-        pl.semaphore_signal(barrier, inc=1, device_id=peer, device_id_type=MESH)
-    pl.semaphore_wait(barrier, len(peers))
-
-    last_round = max(nx, ny) // 2
-
-    def tell(r):
-        if 2 <= r <= last_round:
-            for way, p in enumerate(around):
-                pl.semaphore_signal(ready.at[way, r - 2], inc=1, device_id=(g, p), device_id_type=MESH)
-
-    def hear(r):
-        if 2 <= r <= last_round:
-            for way in range(4):
-                pl.semaphore_wait(ready.at[way, r - 2], 1)
+    up_g, down_g = jnp.minimum(g + 1, ng - 1), jnp.maximum(g - 1, 0)
+    greet((up_g, s), (g < ng - 1) & jnp.logical_not(device0))
+    greet((down_g, s), g > 0)
+    for p in around:
+        greet((g, p), jnp.logical_not(late0))
+    greet((g, 0), (line_y & (y > 1) & (y < ny - 1)) | (line_x & (x > 1) & (x < nx - 1)))
+    awaited = (g < ng - 1).astype(jnp.int32) + ((g > 0) & jnp.logical_not((g == 1) & slab0)).astype(jnp.int32)
+    for p in around:
+        awaited = awaited + jnp.logical_not(late & (p == 0)).astype(jnp.int32)
+    awaited = awaited + jnp.where(late0, ny + nx - 6, 0)
+    pl.semaphore_wait(barrier, awaited)
+
+    @pl.when(device0)
+    def _():
+        pl.semaphore_signal(hello.at[0], inc=1, device_id=(up_g, s), device_id_type=MESH)
+
+    def chain_rounds(axis):
+        p, n, line = (y, ny, line_y) if axis == 0 else (x, nx, line_x)
+
+        def known(q, r, up):
+            on_line = (q - r >= 1) if up else (q + r <= n - 1)
+            return jnp.where(line, on_line & (q > 0), r <= n // 2)
+
+        def tell(r):
+            for way, up in ((0, True), (1, False)):
+                q = lax.rem(p + (1 if up else n - 1), n)
+                good = known(q, r, up) & jnp.logical_not(line & (p == 0))
+
+                @pl.when(good)
+                def _():
+                    to = around[2 * axis + way]
+                    pl.semaphore_signal(ready.at[2 * axis + way, r - 2], inc=1, device_id=(g, to), device_id_type=MESH)
+
+        def hear(r, cond):
+            for way, up in ((0, True), (1, False)):
+                @pl.when(known(p, r, up) & cond)
+                def _():
+                    pl.semaphore_wait(ready.at[2 * axis + way, r - 2], 1)
+
+        return tell, hear
+
+    tell_y, hear_y = chain_rounds(0)
+    tell_x, hear_x = chain_rounds(1)
+    always = s >= 0
+    last_y, last_x = max(ny - 2, 1), max(nx - 2, 1)
 
     regions = [
         (pl.ds(0, NB), pl.ds(0, orb)),
@@ -121,11 +164,20 @@
         def _():
             halo(0, part).start()
 
-        @pl.when(g > 0)
+        @pl.when((g > 0) & jnp.logical_not((g == 1) & slab0))
         def _():
             halo(1, part).start()
 
-    tell(2)
+    if last_y >= 2:
+        tell_y(2)
+    if last_x >= 2:
+        tell_x(2)
+
+    @pl.when((g == 1) & slab0)
+    def _():
+        pl.semaphore_wait(hello.at[0], 1)
+        for part in range(3):
+            halo(1, part).start()
 
     @pl.when(g == 0)
     def _():
@@ -153,8 +205,13 @@
         return 0
 
     lax.fori_loop(0, orb // 16, coef_rows, 0)
-    hear(2)
-    tell(3)
+    def round_y(r):
+        if r <= last_y:
+            hear_y(r, always)
+        if r + 1 <= last_y:
+            tell_y(r + 1)
+
+    round_y(2)
 
     face_row = jnp.concatenate([face[0].astype(F32), face[1].astype(F32)], 1)
     facev[...] = jnp.concatenate([face_row, times_i(face_row)], 0).astype(BF)
@@ -172,8 +229,7 @@
         inverse.append((jnp.where(inner, offset / denom, 0.0), jnp.where(inner, -ETA / denom, 0.0)))
 
     own_copy.wait()
-    hear(3)
-    tell(4)
+    round_y(3)
 
     def halo_wait(part):
         @pl.when(g > 0)
@@ -216,9 +272,37 @@
         bound = pair[0:NB] - (prod[0:NB] + times_i(prod[NB:]))
         brow[e, y] = bound.astype(BF)
 
-    for r in range(4, last_round + 1):
-        hear(r)
-        tell(r + 1)
+    for r in range(4, last_y + 1):
+        round_y(r)
+
+    def first_send(k):
+        to = slab_x(k + 1) if k < nx - 1 else slab_y(k - nx + 2)
+        return pltpu.make_async_remote_copy(
+            src_ref=brow.at[:, 0],
+            dst_ref=first_b,
+            send_sem=first_s.at[k],
+            recv_sem=first_r.at[0],
+            device_id=(g, to),
+            device_id_type=MESH,
+        )
+
+    def first_pass(d):
+        return pltpu.make_async_remote_copy(
+            src_ref=first_b,
+            dst_ref=first_b,
+            send_sem=first_s.at[d - 1],
+            recv_sem=first_r.at[0],
+            device_id=(g, slab_y(d)),
+            device_id_type=MESH,
+        )
+
+    @pl.when(late0)
+    def _():
+        for k in sorted(range(nx - 1), key=lambda k: -min(k + 1, nx - 1 - k)):
+            first_send(k).start()
+        for k in range(nx - 1, nx + ny - 2):
+            first_send(k).start()
+        first_b[...] = brow[:, 0]
 
     far_first = lambda n: sorted(range(1, n), key=lambda d: -min(d, n - d))
 
@@ -245,15 +329,32 @@
             device_id_type=MESH,
         ).wait_recv()
 
+    def sends_first(d):
+        return jnp.logical_not(late0 | (late & (lax.rem(y + d, ny) == 0)))
+
+    def sends_second(d):
+        return (y + d < ny) & jnp.logical_not(late0)
+
     for d in far_first(ny):
-        row_send(d, True).start()
+        @pl.when(sends_first(d))
+        def _():
+            row_send(d, True).start()
+
     for d in far_first(ny):
-        @pl.when(y + d < ny)
+        @pl.when(sends_second(d))
         def _():
             row_send(d, False).start()
 
+    def round_x(r):
+        if r <= last_x:
+            hear_x(r, jnp.logical_not(late0))
+        if r + 1 <= last_x:
+            tell_x(r + 1)
+
+    round_x(2)
     halo_wait(2)
     sigma_region(NB, orb - NB, pl.ds(2 * NB, orb - 2 * NB))
+    round_x(3)
     rv_copy.wait()
     for e in range(2):
         rr, ri = rv[e, 0], rv[e, 1]
@@ -266,6 +367,9 @@
         lesser[e, 0, 0] = (dot_t(hr, rr) + dot_t(hi, ri)).astype(BF)
         lesser[e, 0, 1] = (dot_t(hi, rr) - dot_t(hr, ri)).astype(BF)
 
+    for r in range(4, last_x + 1):
+        round_x(r)
+
     scale = 1.0 / (8.0 * math.sqrt(NB * nx * ny))
     eye = eye_pair()
 
@@ -279,9 +383,17 @@
             blocks = pairs + blocks[len(blocks) - len(blocks) % 2 :]
         return blocks[0]
 
+    def used(i):
+        return jnp.logical_not(line_y) if i == 0 else always
+
     for d in range(1, ny):
-        row_wait(lax.rem(y + d, ny), True)
-    tcol[x] = ordered_product(factors(mine))
+        source = lax.rem(y + d, ny)
+
+        @pl.when(jnp.logical_not(line_x | (line_y & (source == 0))))
+        def _():
+            row_wait(source, True)
+
+    tcol[x] = ordered_product([jnp.where(used(i), f, eye) for i, f in enumerate(factors(mine))])
 
     def total_send(d):
         return pltpu.make_async_remote_copy(
@@ -293,20 +405,41 @@
             device_id_type=MESH,
         )
 
+    def sends_total(d):
+        return (x + d < nx) & jnp.logical_not(line_x)
+
     for d in far_first(nx):
-        @pl.when(x + d < nx)
+        @pl.when(sends_total(d))
         def _():
             total_send(d).start()
 
     for d in range(1, ny):
-        @pl.when(y - d >= 0)
+        @pl.when((y - d >= 0) & jnp.logical_not(line_y & (y == d)))
         def _():
             row_wait(lax.rem(y - d + ny, ny), False)
     for e in range(2):
-        pre[e] = ordered_product([jnp.where(i <= y, f, eye) for i, f in enumerate(factors(e))])
+        pre[e] = ordered_product([jnp.where((i <= y) & used(i), f, eye) for i, f in enumerate(factors(e))])
+
+    def first_wait():
+        pltpu.make_async_remote_copy(
+            src_ref=first_b,
+            dst_ref=first_b,
+            send_sem=first_s.at[0],
+            recv_sem=first_r.at[0],
+            device_id=(g, slab_y(1)),
+            device_id_type=MESH,
+        ).wait_recv()
+
+    passing = line_x & (x > 0)
+
+    @pl.when(passing)
+    def _():
+        first_wait()
+        for d in far_first(ny):
+            first_pass(d).start()
 
     for d in range(1, nx):
-        @pl.when(x - d >= 0)
+        @pl.when((x - d >= 0) & jnp.logical_not(line_x))
         def _():
             source = lax.rem(x - d + nx, nx)
             pltpu.make_async_remote_copy(
@@ -317,23 +450,56 @@
                 device_id=(g, slab_x(1)),
                 device_id_type=MESH,
             ).wait_recv()
-    swap[0] = ordered_product([jnp.where(i < x, tcol[i], eye) for i in range(nx - 1)])
-    swap_copy = pltpu.make_async_remote_copy(
-        src_ref=swap.at[0],
-        dst_ref=swap.at[1],
-        send_sem=swap_s.at[0],
-        recv_sem=swap_r.at[0],
-        device_id=(g, slab_y(1 - 2 * mine)),
-        device_id_type=MESH,
-    )
-    swap_copy.start()
-
-    def finish(e, rows_before):
-        whole = cmul(rows_before, pre[e])
+
+    def swap_copy(k):
+        to = slab_y(1 - 2 * mine) if k == 0 else slab_y(-k)
+        return pltpu.make_async_remote_copy(
+            src_ref=before.at[mine],
+            dst_ref=before.at[mine],
+            send_sem=swap_s.at[k],
+            recv_sem=swap_r.at[mine],
+            device_id=(g, to),
+            device_id_type=MESH,
+        )
+
+    swaps = [
+        (x > 0) & jnp.logical_not(line_x),
+        (x > 0) & late & (y == 2),
+        (x > 0) & late & (y == 2),
+    ]
+    rows_before = ordered_product([jnp.where(i < x, tcol[i], eye) for i in range(nx - 1)])
+
+    @pl.when(jnp.logical_not(line_x))
+    def _():
+        before[mine] = rows_before
+
+    for k in range(3):
+        @pl.when(swaps[k])
+        def _():
+            swap_copy(k).start()
+
+    def before_wait(e):
+        pltpu.make_async_remote_copy(
+            src_ref=before.at[e],
+            dst_ref=before.at[e],
+            send_sem=swap_s.at[0],
+            recv_sem=swap_r.at[e],
+            device_id=(g, slab_y(1)),
+            device_id_type=MESH,
+        ).wait_recv()
+
+    def inner_part(e):
+        pre[e] = cmul(jnp.where(x > 0, before[e], eye), pre[e])
+
+    def store(e, whole):
         chain[e, 0, 0] = whole[:, 0:NB]
         chain[e, 0, 1] = pltpu.roll(whole, NB, 1)[:, 0:NB]
 
-    finish(mine, swap[0])
+    @pl.when((x > 0) & line_x)
+    def _():
+        before_wait(mine)
+
+    inner_part(mine)
 
     for part in range(3):
         @pl.when(g < ng - 1)
@@ -345,19 +511,52 @@
             halo(1, part).wait_send()
 
     for d in range(1, ny):
-        row_send(d, True).wait_send()
-
-        @pl.when(y + d < ny)
+        @pl.when(sends_first(d))
+        def _():
+            row_send(d, True).wait_send()
+
+        @pl.when(sends_second(d))
         def _():
             row_send(d, False).wait_send()
 
+        @pl.when(passing)
+        def _():
+            first_pass(d).wait_send()
+
     for d in range(1, nx):
-        @pl.when(x + d < nx)
+        @pl.when(sends_total(d))
         def _():
             total_send(d).wait_send()
 
-    swap_copy.wait()
-    finish(other, swap[1])
+    @pl.when(x > 0)
+    def _():
+        before_wait(other)
+
+    inner_part(other)
+
+    @pl.when(late & jnp.logical_not(slab0 | passing))
+    def _():
+        first_wait()
+
+    @pl.when(late)
+    def _():
+        for e in range(2):
+            store(e, cmul(eye + scale * dot(first_b[e], facev[...]), pre[e]))
+
+    @pl.when(jnp.logical_not(late))
+    def _():
+        for e in range(2):
+            store(e, pre[e])
+
+    for k in range(3):
+        @pl.when(swaps[k])
+        def _():
+            swap_copy(k).wait_send()
+
+    @pl.when(late0)
+    def _():
+        for k in range(nx + ny - 2):
+            first_send(k).wait_send()
 
 
 def solution(mesh, grid=None):
@@ -370,7 +569,7 @@
         smem = pl.BlockSpec(memory_space=pltpu.SMEM)
         vmem = pl.BlockSpec(memory_space=pltpu.VMEM)
         dma = pltpu.SemaphoreType.DMA
-        rounds = max(max(nx, ny) // 2 - 1, 1)
+        rounds = max(max(nx, ny) - 3, 1)
         return pl.pallas_call(
             functools.partial(kernel, ng, nx, ny, orb),
             out_shape=(
@@ -392,15 +591,19 @@
                 pltpu.VMEM((2 * NB, 2 * NB), BF),
                 pltpu.VMEM((2, NB, 2 * NB), F32),
                 pltpu.VMEM((2, NB, 2 * NB), F32),
+                pltpu.VMEM((2, NB, 2 * NB), BF),
                 dma((4,)),
                 pltpu.SemaphoreType.REGULAR((4, rounds)),
+                pltpu.SemaphoreType.REGULAR((1,)),
                 dma((2, 3)),
                 dma((2, 3)),
                 dma((2, ny - 1)),
                 dma((2, ny)),
                 dma((nx - 1,)),
                 dma((nx,)),
-                dma((1,)),
+                dma((3,)),
+                dma((2,)),
+                dma((nx + ny - 2,)),
                 dma((1,)),
             ],
             compiler_params=pltpu.CompilerParams(collective_id=0, has_side_effects=True),

time: 42.9 us -> 34.3 us (0.80)
  the two profiles are of different devices: /device:TPU:14 before, /device:TPU:524 now
where the time goes in v2:
time: 34.3 us; the launch traced here: 34.1 us
  Pallas kernels  32 us (93%)
  local copies, waits for them, and re-layouts  1.45 us (4%)
  between operations  0.64 us (2%)
    pallas_call x1, Pallas kernels, on_device(): pl.pallas_call(functools.partial(kernel, ng, nx, ny, orb), out_shape=(plt...  32 us
    unnamed x2, local copies, waits for them, and re-layouts  1.45 us

profile of v2, /device:TPU:524, one launch (start us, length us, event | category | flops | bytes accessed | tf_op | source)
XLA Modules:
  0.0 34.1 jit_solution(6264711701733742123)
XLA Ops:
  0.6 32.0 %shard_map.86 = (bf16[2,1,2,256,256]{4,3,2,1,0:T(8,128)(2,1)S(1)}, f32[2,1,2,64,64]{4,3,2,1,0:T(8,128)S(1)}) custom-call(bf16[2,1,2,256,256]{4,3,2,1,0:T(8,128)(2,1)} %less.1, bf16[2,1,2,256,256]{4,3,2,1,0:T(8,128)(2,1)} %ret.1, bf16[1,256,256]{2,1,0:T(8,128)(2,1)} %ham.1, bf16[4,256,256]{2,1,0:T(8,128)(2,1)} %coup.1, f32[4]{0:T(128)} %occ.1, s32[4]{0:T(128)} %shf.1, ...), custom_call_target="tpu_custom_call" | custom-call | tf_op jit(solution)/shard_map/pallas_call | solution.py:573
  32.6 0.8 %copy.11 = bf16[2,1,2,256,256]{4,3,2,1,0:T(8,128)(2,1)} copy(bf16[2,1,2,256,256]{4,3,2,1,0:T(8,128)(2,1)S(1)} %get-tuple-element.2) | data formatting | bytes 1048576
  33.4 0.7 %copy.12 = f32[2,1,2,64,64]{4,3,2,1,0:T(8,128)} copy(f32[2,1,2,64,64]{4,3,2,1,0:T(8,128)S(1)} %get-tuple-element.3) | data formatting | bytes 131072
